TPU v7x, 512 devices: a whole 4x8x8 slice. The times are simulated.
512 devices in a mesh: wide: 128 (over y, z, core), pair: 4 (over x).
Axes of the slice: x: 4, y: 8, z: 8, core: 2. Of those that a mesh axis runs over, the one named last changes fastest.
Arguments:
- blocks: bfloat16 [2048, 1024, 512], P('pair', 'wide'), may hold values from -6 to 6
- basis_a: bfloat16 [1024, 64], replicated, may hold values from -0.1875 to 0.1875
- basis_b: bfloat16 [512, 64], replicated, may hold values from -0.25 to 0.25
- sketch: bfloat16 [2048, 64], P(('pair', 'wide')), may hold values from -6 to 6
Outputs:
- transfer: float32 [4096, 64], P(('wide', 'pair'))
- coefficients: float32 [2048, 64], P(('pair', 'wide'))
All inputs are finite; a program needn't handle non-finite values.
Results may differ from a plain program's by a relative error of at most 0.0041.
Values may be sent and summed in bfloat16 or wider, within the bound.
A program may use at most 64 MiB of HBM per device.

v0:
```python
import jax
import jax.numpy as jnp
from jax import lax
from jax.sharding import PartitionSpec as P


def orthonormal(sketched, gram):
    lower = jnp.linalg.cholesky(gram)
    return lax.linalg.triangular_solve(
        lower, sketched, left_side=False, lower=True, transpose_a=True
    )


def per_device(blocks, basis_a, basis_b, sketch):
    fibres = sketch.shape[0]
    rank_a = basis_a.shape[1]
    rank_b = basis_b.shape[1]
    narrowed = jnp.einsum(
        "fac,cr->far", blocks, basis_b, preferred_element_type=jnp.float32
    ).astype(jnp.bfloat16)
    regrouped = lax.all_to_all(narrowed, "wide", split_axis=0, concat_axis=1, tiled=True)
    projected = jnp.einsum(
        "ap,far->fpr", basis_a, regrouped, preferred_element_type=jnp.float32
    ).astype(jnp.bfloat16)
    projected = projected.reshape(fibres, rank_a * rank_b)
    partial_value = jnp.einsum("fj,fk->jk", projected, sketch, preferred_element_type=jnp.float32)
    own_count = rank_a * rank_b // lax.axis_size(("wide", "pair"))
    sketch_all = lax.psum(partial_value, ("wide", "pair"))
    gram_matrix = jnp.dot(sketch_all.T, sketch_all, precision=lax.Precision.HIGHEST)
    parent_basis = orthonormal(sketch_all, gram_matrix)
    first_row = lax.axis_index(("wide", "pair")) * own_count
    own_basis = lax.dynamic_slice_in_dim(parent_basis, first_row, own_count, 0)
    transfer = own_basis * jnp.sqrt(jnp.float32(rank_a * rank_b))
    coefficients = jnp.dot(
        projected.astype(jnp.float32), parent_basis, precision=lax.Precision.HIGHEST
    )
    return (transfer, coefficients)


def solution(mesh):
    placed = (P("pair", "wide", None), P(), P(), P(("pair", "wide"), None))
    return jax.shard_map(
        per_device,
        mesh=mesh,
        in_specs=placed,
        out_specs=(P(("wide", "pair"), None), P(("pair", "wide"), None)),
        check_vma=False,
    )
```

profile of v0, /device:TPU:24, one launch (start us, length us, event | category | flops | bytes accessed | tf_op | source)
XLA Modules:
  0.0 346.8 jit_solution(4763148819996868437)
XLA Ops:
  7.2 0.0 copy-start
  7.2 0.0 all-reduce.2.cloned.1.call-start
  7.2 3.4 convolution_convert_fusion
  10.7 0.0 copy-start.1
  10.7 0.6 reshape.19
  11.3 35.6 %all_to_all.18 = bf16[128,2,1024]{2,1,0:T(2,128)(2,1)S(1)} all-to-all(bf16[128,2,1024]{2,1,0:T(2,128)(2,1)S(1)} %reshape.19), channel_id=1, replica_groups=mesh['wide'=128,'pair'=4] {'wide'}, dimensions={0} | all-to-all | bytes 1048576 | tf_op jit(solution)/shard_map/all_to_all | solution.py:21
  46.9 0.6 reshape.20
  47.5 0.0 copy-done
  47.5 0.5 fusion
  48.0 0.1 copy.19
  48.1 0.1 reshape.16
  48.2 0.0 copy-done.1
  48.2 1.4 fusion.9
  49.6 0.0 all-reduce.2.cloned.1.call-update
  49.6 271.4 %all-reduce.2.cloned.1.call-done = f32[4096,64]{0,1:T(8,128)} async-done(((f32[4096,64]{0,1:T(8,128)}), f32[4096,64]{0,1:T(8,128)}) %all-reduce.2.cloned.1.call-update) | async-done | bytes 1048592 | tf_op jit(solution)/shard_map/psum | solution.py:28
  321.0 2.5 fusion.10
  323.5 0.1 copy.20
  323.6 5.8 %cholesky.16 = f32[64,64]{1,0:T(8,128)S(1)} custom-call(f32[64,64]{1,0:T(8,128)S(1)} %fusion.8), custom_call_target="Cholesky" | custom-call | tf_op jit(solution)/shard_map/jit(cholesky)/cholesky | solution.py:8
  329.5 0.6 compare_reduce_fusion
  330.2 0.7 fusion.5
  330.8 4.9 %custom-call.6 = f32[1,64,64]{1,2,0:T(8,128)S(1)} custom-call(f32[1,64,64]{2,1,0:T(8,128)S(1)} %fusion.5), custom_call_target="InvertDiagBlocksLowerTriangular" | custom-call | tf_op jit(solution)/shard_map/triangular_solve | solution.py:9
  335.7 2.3 fusion.6
  338.0 1.2 fusion.11
  339.2 0.1 dynamic-slice_multiply_fusion
  339.3 0.7 copy.21
  (2 shorter events, 0.0 us)
Async XLA Ops:
  7.2 40.3 %copy-start = (bf16[1024,64]{0,1:T(8,128)(2,1)S(1)}, bf16[1024,64]{0,1:T(8,128)(2,1)}, u32[]{:S(2)}) copy-start(bf16[1024,64]{0,1:T(8,128)(2,1)} %param.5) | copy-start | bytes 393220
  7.2 313.8 %all-reduce.2.cloned.1.call-start = ((), (), s32[]{:S(2)}) async-start(), calls=%async_computation.1 | async-start | bytes 2097152 | tf_op jit(solution)/shard_map/psum | solution.py:28
  10.7 37.5 %copy-start.1 = (bf16[4,64]{1,0:T(4,128)(2,1)S(1)}, bf16[4,64]{1,0:T(4,128)(2,1)}, u32[]{:S(2)}) copy-start(bf16[4,64]{1,0:T(4,128)(2,1)} %param.7) | copy-start | bytes 1540
Sparse Core Ops, SparseCore 0:
  49.7 271.2 all-reduce.1
where the time goes:
time: 347 us
  waiting for transfers between devices  271 us (78%)
  blocking collectives  35.6 us (10%)
  between operations  14.1 us (4%)
  other arithmetic  12.2 us (4%)
  matrix products  11.3 us (3%)
    psum x1, waiting for transfers between devices, per_device(): sketch_all = lax.psum(partial_value, ('wide', 'pair'))  271 us
    all_to_all x1, blocking collectives, per_device(): lax.all_to_all(narrowed, 'wide', split_axis=0, concat_axis=1, tiled=True)  35.6 us
  transfers between devices with their start and end apart: 1, of which 1 were waited for; matrix products, arithmetic and copies ran while one was open for 0% of the time, Pallas kernels for 0%

commit v1 on v0

--- a/solution.py
+++ b/solution.py
@@ -25,7 +25,7 @@
     projected = projected.reshape(fibres, rank_a * rank_b)
     partial_value = jnp.einsum("fj,fk->jk", projected, sketch, preferred_element_type=jnp.float32)
     own_count = rank_a * rank_b // lax.axis_size(("wide", "pair"))
-    sketch_all = lax.psum(partial_value, ("wide", "pair"))
+    sketch_all = lax.psum(lax.psum(partial_value, "wide"), "pair")
     gram_matrix = jnp.dot(sketch_all.T, sketch_all, precision=lax.Precision.HIGHEST)
     parent_basis = orthonormal(sketch_all, gram_matrix)
     first_row = lax.axis_index(("wide", "pair")) * own_count

time: 347 us -> 325 us (0.937)
  the two profiles are of different devices: /device:TPU:24 before, /device:TPU:8 now
where the time goes in v1:
time: 325 us; the launch traced here: 324 us
  waiting for transfers between devices  247 us (76%)
  blocking collectives  37.5 us (12%)
  between operations  14.2 us (4%)
  other arithmetic  12.2 us (4%)
  matrix products  11.4 us (4%)
    psum x2, waiting for transfers between devices, per_device(): sketch_all = lax.psum(lax.psum(partial_value, 'wide'), 'pair')  247 us
    all_to_all x1, blocking collectives, per_device(): lax.all_to_all(narrowed, 'wide', split_axis=0, concat_axis=1, tiled=True)  37.5 us
    another operation x3, other arithmetic, orthonormal(): lower = jnp.linalg.cholesky(gram)  6.52 us
  transfers between devices with their start and end apart: 2, of which 2 were waited for; matrix products, arithmetic and copies ran while one was open for 0% of the time, Pallas kernels for 0%

profile of v1, /device:TPU:8, one launch (start us, length us, event | category | flops | bytes accessed | tf_op | source)
XLA Modules:
  0.0 324.4 jit_solution(1043105510741689203)
XLA Ops:
  7.2 0.0 copy-start
  7.2 0.0 all-reduce.3.cloned.1.call-start
  7.2 3.4 %convolution_convert_fusion = bf16[512,8,64]{2,1,0:T(8,128)(2,1)S(1)} fusion(bf16[512,8,512]{2,1,0:T(8,128)(2,1)} %param.4, bf16[512,64]{0,1:T(8,128)(2,1)} %param.6), kind=kOutput, calls=%fused_computation | convolution fusion | flops 268697600 | bytes 4784128 | tf_op jit(solution)/shard_map/fac,cr->far/dot_general | solution.py:18
  10.7 0.0 copy-start.1
  10.7 0.6 reshape.19
  11.3 37.5 %all_to_all.18 = bf16[128,2,1024]{2,1,0:T(2,128)(2,1)S(1)} all-to-all(bf16[128,2,1024]{2,1,0:T(2,128)(2,1)S(1)} %reshape.19), channel_id=1, replica_groups=mesh['wide'=128,'pair'=4] {'wide'}, dimensions={0} | all-to-all | bytes 1048576 | tf_op jit(solution)/shard_map/all_to_all | solution.py:21
  48.7 0.6 reshape.20
  49.3 0.0 copy-done
  49.4 0.5 fusion
  49.9 0.1 copy.19
  50.0 0.1 reshape.16
  50.1 0.0 copy-done.1
  50.1 1.4 fusion.9
  51.5 0.0 all-reduce.3.cloned.1.call-update
  51.5 0.0 all-reduce.5.cloned.1.call-start
  51.5 190.0 %all-reduce.3.cloned.1.call-done = f32[4096,64]{0,1:T(8,128)} async-done(((f32[4096,64]{0,1:T(8,128)}), f32[4096,64]{0,1:T(8,128)}) %all-reduce.3.cloned.1.call-update) | async-done | bytes 1048592 | tf_op jit(solution)/shard_map/psum | solution.py:28
  241.5 0.0 all-reduce.5.cloned.1.call-update
  241.6 57.0 %all-reduce.5.cloned.1.call-done = f32[4096,64]{0,1:T(8,128)} async-done(((f32[4096,64]{0,1:T(8,128)}), f32[4096,64]{0,1:T(8,128)}) %all-reduce.5.cloned.1.call-update) | async-done | bytes 1048592 | tf_op jit(solution)/shard_map/psum | solution.py:28
  298.5 2.6 fusion.10
  301.2 0.1 copy.20
  301.3 5.8 %cholesky.16 = f32[64,64]{1,0:T(8,128)S(1)} custom-call(f32[64,64]{1,0:T(8,128)S(1)} %fusion.8), custom_call_target="Cholesky" | custom-call | tf_op jit(solution)/shard_map/jit(cholesky)/cholesky | solution.py:8
  307.2 0.6 compare_reduce_fusion
  307.8 0.7 fusion.5
  308.5 4.9 %custom-call.6 = f32[1,64,64]{1,2,0:T(8,128)S(1)} custom-call(f32[1,64,64]{2,1,0:T(8,128)S(1)} %fusion.5), custom_call_target="InvertDiagBlocksLowerTriangular" | custom-call | tf_op jit(solution)/shard_map/triangular_solve | solution.py:9
  313.4 2.3 fusion.6
  315.6 1.2 fusion.11
  316.8 0.1 dynamic-slice_multiply_fusion
  316.9 0.7 copy.21
  (2 shorter events, 0.0 us)
Async XLA Ops:
  7.2 42.2 %copy-start = (bf16[1024,64]{0,1:T(8,128)(2,1)S(1)}, bf16[1024,64]{0,1:T(8,128)(2,1)}, u32[]{:S(2)}) copy-start(bf16[1024,64]{0,1:T(8,128)(2,1)} %param.5) | copy-start | bytes 393220
  7.2 234.4 %all-reduce.3.cloned.1.call-start = ((), (), s32[]{:S(2)}) async-start(), calls=%async_computation.1 | async-start | bytes 2097152 | tf_op jit(solution)/shard_map/psum | solution.py:28
  10.7 39.4 %copy-start.1 = (bf16[4,64]{1,0:T(4,128)(2,1)S(1)}, bf16[4,64]{1,0:T(4,128)(2,1)}, u32[]{:S(2)}) copy-start(bf16[4,64]{1,0:T(4,128)(2,1)} %param.7) | copy-start | bytes 1540
  51.5 247.0 %all-reduce.5.cloned.1.call-start = ((), (), s32[]{:S(2)}) async-start(), calls=%async_computation.2 | async-start | bytes 2097152 | tf_op jit(solution)/shard_map/psum | solution.py:28
Sparse Core Ops, SparseCore 0:
  51.6 189.8 all-reduce.2
  243.9 54.5 all-reduce.4
